TPU v7x, 256 devices: a whole 4x4x8 slice. The times are simulated.
256 devices in a mesh: ctx: 16 (over z, core), exp: 16 (over x, y).
Axes of the slice: x: 4, y: 4, z: 8, core: 2. Of those that a mesh axis runs over, the one named last changes fastest.
Arguments:
- queries: bfloat16 [2, 16384, 2560], P(None, ('ctx', 'exp'))
- key_states: bfloat16 [2, 16384, 512], P(None, ('ctx', 'exp'))
- value_state_rows: bfloat16 [2, 16384, 512], P(None, ('ctx', 'exp')), may hold values from -6 to 6
- block_lists: int32 [32], replicated, may hold values from 0 to 31, as said below
- hidden: bfloat16 [8192, 5120], P(('ctx', 'exp')), may hold values from -8 to 8
- router: bfloat16 [5120, 16], replicated, may hold values from -0.078125 to 0.078125
- expert_ids: int32 [8192, 1], P(('ctx', 'exp')), may hold values from 0 to 15; in each aligned block of 32 rows (0 to 31, 32 to 63, ...) at most 4 rows name the same one
- w_gate: bfloat16 [16, 5120, 4096], P('exp', None, 'ctx'), may hold values from -0.078125 to 0.078125
- w_up: bfloat16 [16, 5120, 4096], P('exp', None, 'ctx'), may hold values from -0.078125 to 0.078125
- w_down: bfloat16 [16, 4096, 5120], P('exp', 'ctx'), may hold values from -0.1875 to 0.1875
Outputs:
- attention: bfloat16 [2, 16384, 2560], P(None, ('ctx', 'exp'))
- moe_out: bfloat16 [8192, 5120], P(('ctx', 'exp'))
Inputs may be any that keep to these rules, and one draw needn't show every extreme that they name: block_lists[b] is a block before b, or b itself when block b attends only to its own keys (always for b = 0 and for b = 31). Block p is held by index min(p, 31 - p) of ctx; for each d < 16 with block_lists[d] != d and block_lists[31 - d] != 31 - d, the two listed blocks are held by different indices. `expert_ids`: among the rows of one device no expert is named more than 4 times.
All inputs are finite; a program needn't handle non-finite values.
Results may differ from a plain program's by a relative error of at most 0.023.
Values may be sent and summed in bfloat16 or wider, within the bound.
No kernel may reach another device: no remote copies, remote signals or barrier semaphores. Data moves between devices by JAX's collectives and lax.ppermute only.
A program may use at most 128 MiB of HBM per device.

v0:
```python
import jax
import jax.numpy as jnp
from jax import lax
from jax.sharding import PartitionSpec as P

QUERY_HEADS = 20
KEY_HEADS = 4
HEAD_DIM = 128
NEGATIVE_LARGE = -1e30


def attend_all(queries, key_states, value_state_rows, block_lists):
    ctx_count = lax.axis_size("ctx")
    blocks_total = 2 * ctx_count
    ctx_index = lax.axis_index("ctx")
    exp_index = lax.axis_index("exp")
    row_total_count = queries.shape[1]
    query_group_width = QUERY_HEADS // KEY_HEADS
    key_value_width = KEY_HEADS * HEAD_DIM
    paired = jnp.concatenate([key_states, value_state_rows], axis=2)
    own_blocks = jnp.stack([ctx_index, blocks_total - 1 - ctx_index])
    listed = block_lists[own_blocks]
    usable = listed != own_blocks
    holder = jnp.minimum(listed, blocks_total - 1 - listed)
    everyone = lax.all_gather(paired[None], "ctx", axis=0, tiled=True)
    second_half = (listed >= ctx_count).astype(jnp.int32)
    remote = everyone[holder, second_half]
    stacked = jnp.concatenate([paired, remote], axis=0)
    query_head_rows = queries.reshape(2, row_total_count, KEY_HEADS, query_group_width, HEAD_DIM)
    query_pos = exp_index * row_total_count + jnp.arange(row_total_count)
    scaling = HEAD_DIM ** (-0.5)
    piece_rows = lax.all_gather(stacked, "exp", axis=1, tiled=True)
    running_maximum = jnp.full(
        (2, KEY_HEADS, query_group_width, row_total_count), NEGATIVE_LARGE, jnp.float32
    )
    key_total_count = piece_rows.shape[1]
    concatenated_rows = jnp.concatenate([piece_rows[0:2], piece_rows[2:4]], axis=1)
    key_portion = concatenated_rows[..., :key_value_width].reshape(
        2, 2 * key_total_count, KEY_HEADS, HEAD_DIM
    )
    value_portion = concatenated_rows[..., key_value_width:].reshape(
        2, 2 * key_total_count, KEY_HEADS, HEAD_DIM
    )
    scores = (
        jnp.einsum(
            "prhgd,pkhd->phgrk", query_head_rows, key_portion, preferred_element_type=jnp.float32
        )
        * scaling
    )
    key_pos = jnp.arange(key_total_count)
    causal = jnp.broadcast_to(
        (key_pos[None, :] <= query_pos[:, None])[None], (2, row_total_count, key_total_count)
    )
    listed_ok = jnp.broadcast_to(usable[:, None, None], (2, row_total_count, key_total_count))
    allowed = jnp.concatenate([causal, listed_ok], axis=2)[:, None, None]
    masked = jnp.where(allowed, scores, NEGATIVE_LARGE)
    new_max = jnp.maximum(running_maximum, jnp.max(masked, axis=-1))
    weights = jnp.where(allowed, jnp.exp(masked - new_max[..., None]), 0.0)
    new_sum = jnp.sum(weights, axis=-1)
    update = jnp.einsum(
        "phgrk,pkhd->phgrd",
        weights.astype(jnp.bfloat16),
        value_portion,
        preferred_element_type=jnp.float32,
    )
    mixed_rows = update / new_sum[..., None]
    return (
        jnp.transpose(mixed_rows, (0, 3, 1, 2, 4))
        .reshape(2, row_total_count, QUERY_HEADS * HEAD_DIM)
        .astype(jnp.bfloat16)
    )


def route_experts(hidden, router, expert_ids, w_gate, w_up, w_down):
    expert_table = router.shape[1]
    local_tokens = hidden.shape[0]
    model_width = hidden.shape[1]
    capacity = max(2, 2 * local_tokens // expert_table)
    exp_count = lax.axis_size("exp")
    logits = jnp.dot(hidden, router, preferred_element_type=jnp.float32)
    selected_expert = expert_ids[:, 0]
    onehot = (selected_expert[:, None] == jnp.arange(expert_table)[None, :]).astype(jnp.float32)
    gate_score = jax.nn.sigmoid(jnp.sum(logits * onehot, axis=1))
    scaled_scores = (hidden.astype(jnp.float32) * gate_score[:, None]).astype(jnp.bfloat16)
    slot_rank = (jnp.sum(jnp.cumsum(onehot, axis=0) * onehot, axis=1) - 1.0).astype(jnp.int32)
    dispatch = (
        (selected_expert[None, None, :] == jnp.arange(expert_table)[:, None, None])
        & (slot_rank[None, None, :] == jnp.arange(capacity)[None, :, None])
    ).astype(jnp.bfloat16)
    gate_local = w_gate[0]
    up_local = w_up[0]
    down_local = w_down[0]
    outgoing = jnp.einsum(
        "ect,td->ecd", dispatch, scaled_scores, preferred_element_type=jnp.float32
    ).astype(jnp.bfloat16)
    incoming = lax.all_to_all(outgoing, "exp", split_axis=0, concat_axis=0, tiled=True)
    piece_rows = lax.all_gather(incoming.reshape(-1, model_width), "ctx", axis=0, tiled=True)
    gate_part = jnp.dot(piece_rows, gate_local, preferred_element_type=jnp.float32)
    up_part = jnp.dot(piece_rows, up_local, preferred_element_type=jnp.float32)
    hidden_activation = (jax.nn.silu(gate_part) * up_part).astype(jnp.bfloat16)
    summed_output = lax.psum_scatter(
        jnp.dot(hidden_activation, down_local, preferred_element_type=jnp.float32).astype(
            jnp.bfloat16
        ),
        "ctx",
        scatter_dimension=0,
        tiled=True,
    )
    returned = lax.all_to_all(
        summed_output.reshape(exp_count, capacity, model_width),
        "exp",
        split_axis=0,
        concat_axis=0,
        tiled=True,
    )
    return jnp.einsum("ect,ecd->td", dispatch, returned, preferred_element_type=jnp.float32).astype(
        jnp.bfloat16
    )


def shards(
    queries,
    key_states,
    value_state_rows,
    block_lists,
    hidden,
    router,
    expert_ids,
    w_gate,
    w_up,
    w_down,
):
    attention = attend_all(queries, key_states, value_state_rows, block_lists)
    moe_out = route_experts(hidden, router, expert_ids, w_gate, w_up, w_down)
    return (attention, moe_out)


def solution(mesh):
    placed = (
        P(None, ("ctx", "exp"), None),
        P(None, ("ctx", "exp"), None),
        P(None, ("ctx", "exp"), None),
        P(),
        P(("ctx", "exp"), None),
        P(),
        P(("ctx", "exp"), None),
        P("exp", None, "ctx"),
        P("exp", None, "ctx"),
        P("exp", "ctx", None),
    )
    return jax.shard_map(
        shards,
        mesh=mesh,
        in_specs=placed,
        out_specs=(P(None, ("ctx", "exp"), None), P(("ctx", "exp"), None)),
        check_vma=False,
    )
```

profile of v0, /device:TPU:2, one launch (start us, length us, event | category | flops | bytes accessed | tf_op | source)
XLA Modules:
  0.0 308.0 jit_solution(14980662462300857561)
XLA Ops:
  7.2 1.1 constant_dynamic-update-slice_fusion.1
  11.5 1.3 fusion.24
  13.5 1.4 convolution_convert_fusion.1
  15.4 18.6 %all_to_all.10 = bf16[16,4,5120]{2,1,0:T(4,128)(2,1)S(1)} all-to-all(bf16[16,4,5120]{2,1,0:T(4,128)(2,1)S(1)} %copy.30), channel_id=1, replica_groups=mesh['ctx'=16,'exp'=16] {'exp'}, dimensions={0} | all-to-all | bytes 1310720 | tf_op jit(solution)/shard_map/all_to_all | solution.py:96
  35.2 1.3 gather_fusion
  36.5 19.3 %all-gather.9.cloned.1.call-done = bf16[32,64,1024]{2,1,0:T(8,128)(2,1)} async-done(((bf16[2,64,1024]{2,1,0:T(8,128)(2,1)}), bf16[32,64,1024]{2,1,0:T(8,128)(2,1)}) %all-gather.9.cloned.1.call-update) | async-done | bytes 4194320 | tf_op jit(solution)/shard_map/all_gather | solution.py:25
  55.8 2.8 gather_fusion.1
  58.5 1.8 pad_maximum_fusion.1
  60.4 61.9 %all-gather.7.cloned.1.call-done = bf16[1024,5120]{1,0:T(8,128)(2,1)} async-done(((bf16[64,5120]{1,0:T(8,128)(2,1)}), bf16[1024,5120]{1,0:T(8,128)(2,1)}) %all-gather.7.cloned.1.call-update) | async-done | bytes 10485776 | tf_op jit(solution)/shard_map/all_gather | solution.py:97
  122.3 8.6 %fusion.11 = f32[1024,256]{1,0:T(8,128)} fusion(bf16[1024,5120]{1,0:T(8,128)(2,1)} %all-gather.7.cloned.1.call-done, bf16[1,5120,256]{2,1,0:T(8,128)(2,1)} %param.17), kind=kOutput, calls=%fused_computation.20 | convolution fusion | flops 2684354560 | bytes 14155776 | tf_op jit(solution)/shard_map/dot_general | solution.py:98
  130.9 21.1 %convolution_convert_fusion = bf16[1024,5120]{1,0:T(8,128)(2,1)} fusion(bf16[1,256,5120]{2,1,0:T(8,128)(2,1)S(1)} %copy-done, bf16[1024,5120]{1,0:T(8,128)(2,1)} %all-gather.7.cloned.1.call-done, bf16[1,5120,256]{2,1,0:T(8,128)(2,1)} %param.18, f32[1024,256]{1,0:T(8,128)} %fusion.11), kind=kOutput, calls=%fused_computation.9 | convolution fusion | flops 5375524864 | bytes 27262976 | tf_op jit(solution)/shard_map/dot_general | solution.py:102
  154.2 44.9 %all-gather.5.cloned.1.call-done = bf16[4,1024,1024]{2,1,0:T(8,128)(2,1)} async-done(((bf16[4,64,1024]{2,1,0:T(8,128)(2,1)}), bf16[4,1024,1024]{2,1,0:T(8,128)(2,1)}) %all-gather.5.cloned.1.call-update) | async-done | bytes 8388624 | tf_op jit(solution)/shard_map/all_gather | solution.py:32
  199.1 3.9 %fusion.57 = (bf16[2,1024,1024]{2,1,0:T(8,128)(2,1)S(1)}, bf16[2,1024,1024]{2,1,0:T(8,128)(2,1)S(1)}) fusion(bf16[4,1024,1024]{2,1,0:T(8,128)(2,1)} %all-gather.5.cloned.1.call-done), kind=kLoop, calls=%fused_computation.78 | loop fusion | bytes 16777216 | tf_op jit(solution)/shard_map/slice | solution.py:37
  203.1 3.7 %fusion.7 = (bf16[2,2048,512]{2,1,0:T(8,128)(2,1)}, bf16[2,2048,512]{2,1,0:T(8,128)(2,1)}) fusion(bf16[2,1024,1024]{2,1,0:T(8,128)(2,1)S(1)} %get-tuple-element.4, bf16[2,1024,1024]{2,1,0:T(8,128)(2,1)S(1)} %get-tuple-element.5), kind=kLoop, calls=%fused_computation.15 | loop fusion | flops 16777216 | bytes 16777216 | tf_op jit(solution)/shard_map/concatenate | solution.py:37
  206.8 6.3 %copy.25 = bf16[2,2048,512]{1,2,0:T(8,128)(2,1)} copy(bf16[2,2048,512]{2,1,0:T(8,128)(2,1)} %get-tuple-element.3) | data formatting | bytes 8388608 | tf_op jit(solution)/shard_map/slice | solution.py:41
  213.1 6.3 %copy.22 = bf16[2,2048,512]{1,2,0:T(8,128)(2,1)} copy(bf16[2,2048,512]{2,1,0:T(8,128)(2,1)} %get-tuple-element.2) | data formatting | bytes 8388608 | tf_op jit(solution)/shard_map/slice | solution.py:38
  219.4 13.4 %fusion = (f32[2,4,5,64]{3,2,1,0:T(8,128)S(1)}, f32[2,4,2048,64,5]{2,3,4,1,0:T(8,128)}) fusion(pred[2,64,2048]{2,1,0:T(8,128)(4,1)S(1)} %pad_add_fusion, bf16[2,2048,4,128,1]{1,3,4,2,0:T(8,128)(2,1)} %bitcast.70, bf16[2,64,4,5,128]{4,3,2,1,0:T(8,128)(2,1)S(1)} %reshape.250), kind=kOutput, calls=%fused_computation.4 | convolution fusion | flops 1357903360 | bytes 26093568 | tf_op jit(solution)/shard_map/prhgd,pkhd->phgrk/dot_general | solution.py:45
  232.9 11.6 %fusion.1 = f32[2,4,5,64]{3,2,1,0:T(8,128)} fusion(f32[2,4,2048,64,5]{2,3,4,1,0:T(8,128)} %get-tuple-element.7, f32[2,4,5,64]{3,2,1,0:T(8,128)S(1)} %broadcast_maximum_fusion, pred[2,64,2048]{2,1,0:T(8,128)(4,1)S(1)} %pad_add_fusion), kind=kLoop, calls=%fused_computation.5 | loop fusion | flops 26211840 | bytes 21254144 | tf_op jit(solution)/shard_map/reduce_sum | solution.py:59
  244.5 31.3 %reduce-scatter.2.cloned.1.call-done = bf16[64,5120]{1,0:T(8,128)(2,1)} async-done(((bf16[1024,5120]{1,0:T(8,128)(2,1)}), bf16[64,5120]{1,0:T(8,128)(2,1)}) %reduce-scatter.2.cloned.1.call-update) | async-done | bytes 655376 | tf_op jit(solution)/shard_map/reduce_scatter | solution.py:101
  275.8 2.4 reshape.253
  278.2 7.4 %all-to-all-start.1 = ((bf16[16,4,5120]{2,1,0:T(4,128)(2,1)}), bf16[16,4,5120]{2,1,0:T(4,128)(2,1)S(1)}, u32[]{:S(2)}, u32[]{:S(2)}) async-start(bf16[16,4,5120]{2,1,0:T(4,128)(2,1)} %reshape.253), calls=%async_computation.2 | async-start | bytes 1310720 | tf_op jit(solution)/shard_map/all_to_all | solution.py:109
  285.5 10.9 %divide_convert_fusion = bf16[2,64,4,5,128]{4,1,3,2,0:T(8,128)(2,1)S(1)} fusion(bf16[2,2048,4,128,1]{1,3,4,2,0:T(8,128)(2,1)} %bitcast.71, f32[2,4,2048,64,5]{2,3,4,1,0:T(8,128)} %get-tuple-element.7, f32[2,4,5,64]{3,2,1,0:T(8,128)} %copy-done.4, pred[2,64,2048]{2,1,0:T(8,128)(4,1)S(1)} %pad_add_fusion, f32[2,64,4,5]{1,3,2,0:T(8,128)} %bitcast.72), kind=kOutput, calls=%fused_computation.23 | convolution fusion | flops 1369047040 | bytes 26103808 | tf_op jit(solution)/shard_map/phgrk,pkhd->phgrd/dot_general | solution.py:60
  296.4 1.4 copy.27
  297.9 2.6 convert_element_type.51
  (43 shorter events, 8.9 us)
Async XLA Ops:
  7.2 123.7 %copy-start = (bf16[1,256,5120]{2,1,0:T(8,128)(2,1)S(1)}, bf16[1,256,5120]{2,1,0:T(8,128)(2,1)}, u32[]{:S(2)}) copy-start(bf16[1,256,5120]{2,1,0:T(8,128)(2,1)} %param.19) | copy-start | bytes 7864324
  7.2 48.6 %all-gather.9.cloned.1.call-start = ((), (), s32[]{:S(2)}) async-start(), calls=%async_computation.6 | async-start | bytes 4456448 | tf_op jit(solution)/shard_map/all_gather | solution.py:25
  9.2 0.7 copy-start.2
  9.9 112.4 %all-gather.7.cloned.1.call-start = ((), (), s32[]{:S(2)}) async-start(), calls=%async_computation.4 | async-start | bytes 11141120 | tf_op jit(solution)/shard_map/all_gather | solution.py:97
  35.0 164.1 %all-gather.5.cloned.1.call-start = ((), (), s32[]{:S(2)}) async-start(), calls=%async_computation.3 | async-start | bytes 8912896 | tf_op jit(solution)/shard_map/all_gather | solution.py:32
  60.3 215.5 %reduce-scatter.2.cloned.1.call-start = ((), (), s32[]{:S(2)}) async-start(), calls=%async_computation.5 | async-start | bytes 11141120 | tf_op jit(solution)/shard_map/reduce_scatter | solution.py:101
  152.0 1.1 copy-start.3
  232.9 11.6 %copy-start.4 = (f32[2,4,5,64]{3,2,1,0:T(8,128)}, f32[2,4,5,64]{3,2,1,0:T(8,128)S(1)}, u32[]{:S(2)}) copy-start(f32[2,4,5,64]{3,2,1,0:T(8,128)S(1)} %broadcast_maximum_fusion) | copy-start | bytes 30724
  278.2 22.3 %all-to-all-start.1 = ((bf16[16,4,5120]{2,1,0:T(4,128)(2,1)}), bf16[16,4,5120]{2,1,0:T(4,128)(2,1)S(1)}, u32[]{:S(2)}, u32[]{:S(2)}) async-start(bf16[16,4,5120]{2,1,0:T(4,128)(2,1)} %reshape.253), calls=%async_computation.2 | async-start | bytes 1310720 | tf_op jit(solution)/shard_map/all_to_all | solution.py:109
  285.5 15.9 %copy-start.1 = (bf16[1,256,5120]{2,1,0:T(8,128)(2,1)S(1)}, bf16[1,256,5120]{2,1,0:T(8,128)(2,1)}, u32[]{:S(2)}) copy-start(bf16[1,256,5120]{2,1,0:T(8,128)(2,1)} %param.19) | copy-start | bytes 7864324
Sparse Core Ops, SparseCore 0:
  10.4 45.3 all-gather.8
  58.2 64.0 all-gather.6
  124.8 74.2 all-gather.4
  201.5 74.1 reduce-scatter.1
where the time goes:
time: 309 us; the launch traced here: 308 us
  waiting for transfers between devices  157 us (51%)
  matrix products  57.7 us (19%)
  local copies, waits for them, and re-layouts  33.3 us (11%)
  other arithmetic  19.5 us (6%)
  blocking collectives  18.6 us (6%)
  between operations  13.9 us (4%)
  starting transfers between devices  7.54 us (2%)
    all_gather x1, waiting for transfers between devices, route_experts(): lax.all_gather(incoming.reshape(-1, model_width), 'ctx', axis=0, tiled=True)  61.9 us
    all_gather x1, waiting for transfers between devices, attend_all(): piece_rows = lax.all_gather(stacked, 'exp', axis=1, tiled=True)  44.9 us
    reduce_scatter x1, waiting for transfers between devices, route_experts(): lax.psum_scatter(jnp.dot(hidden_activation, down_local, preferred_element...  31.3 us
    dot_general x1, matrix products, route_experts(): jnp.dot(hidden_activation, down_local, preferred_element_type=jnp.float32)  21.1 us
    all_gather x1, waiting for transfers between devices, attend_all(): everyone = lax.all_gather(paired[None], 'ctx', axis=0, tiled=True)  19.3 us
    all_to_all x1, blocking collectives, route_experts(): lax.all_to_all(outgoing, 'exp', split_axis=0, concat_axis=0, tiled=True)  18.6 us
    dot_general x1, matrix products, attend_all(): jnp.einsum('prhgd,pkhd->phgrk', query_head_rows, key_portion, preferred_e...  13.4 us
    reduce_sum x1, other arithmetic, attend_all(): new_sum = jnp.sum(weights, axis=-1)  11.6 us
  transfers between devices with their start and end apart: 5, of which 4 were waited for; matrix products, arithmetic and copies ran while one was open for 34% of the time, Pallas kernels for 0%

commit v1 on v0

--- a/solution.py
+++ b/solution.py
@@ -1,3 +1,4 @@
+import functools
 import jax
 import jax.numpy as jnp
 from jax import lax
@@ -7,6 +8,19 @@
 KEY_HEADS = 4
 HEAD_DIM = 128
 NEGATIVE_LARGE = -1e30
+
+
+def number_panel(base_x, k_dim):
+    grid = []
+    for _ in range(jax.lax.axis_size("ctx")):
+        grid.append(base_x)
+    response = jnp.stack(grid, 0)
+    arr_now = jax.lax.all_to_all(response, "ctx", 0, 0)
+    w2 = jnp.concatenate(arr_now, k_dim)
+    return w2
+
+
+fit_edge_all = functools.partial(number_panel, k_dim=0)
 
 
 def attend_all(queries, key_states, value_state_rows, block_lists):
@@ -94,7 +108,7 @@
         "ect,td->ecd", dispatch, scaled_scores, preferred_element_type=jnp.float32
     ).astype(jnp.bfloat16)
     incoming = lax.all_to_all(outgoing, "exp", split_axis=0, concat_axis=0, tiled=True)
-    piece_rows = lax.all_gather(incoming.reshape(-1, model_width), "ctx", axis=0, tiled=True)
+    piece_rows = fit_edge_all(incoming.reshape(-1, model_width))
     gate_part = jnp.dot(piece_rows, gate_local, preferred_element_type=jnp.float32)
     up_part = jnp.dot(piece_rows, up_local, preferred_element_type=jnp.float32)
     hidden_activation = (jax.nn.silu(gate_part) * up_part).astype(jnp.bfloat16)

time: 309 us -> 414 us (1.34)
  waiting for transfers between devices: 157 us -> 249 us
  starting transfers between devices: 7.54 us -> 16.2 us
  local copies, waits for them, and re-layouts: 33.3 us -> 39.1 us
    all_to_all x0 -> x1, waiting for transfers between devices: none -> 196 us  [number_panel(): arr_now = jax.lax.all_to_all(response, 'ctx', 0, 0)]
    all_gather x1 -> x0, waiting for transfers between devices: 61.9 us -> none  [route_experts(): lax.all_gather(incoming.reshape(-1, model_width), 'ctx', axis=0, tiled=True)]
    all_gather x1, waiting for transfers between devices: 44.9 us -> 0.02 us  [attend_all(): piece_rows = lax.all_gather(stacked, 'exp', axis=1, tiled=True)]
    all_gather x1, waiting for transfers between devices: 19.3 us -> 29 us  [attend_all(): everyone = lax.all_gather(paired[None], 'ctx', axis=0, tiled=True)]
    all_to_all x0 -> x1, starting transfers between devices: none -> 8.75 us  [number_panel(): arr_now = jax.lax.all_to_all(response, 'ctx', 0, 0)]
    another operation x0 -> x2, local copies, waits for them, and re-layouts: none -> 7.44 us  [number_panel(): response = jnp.stack(grid, 0)]
    reduce_scatter x1, waiting for transfers between devices: 31.3 us -> 24.5 us  [route_experts(): lax.psum_scatter(jnp.dot(hidden_activation, down_local, preferred_element...]
  transfers between devices with their start and end apart: 5 -> 5, of which waited for: 4 -> 3; matrix products, arithmetic and copies ran while one was open for 34% -> 26% of each run, Pallas kernels for 0% -> 0%
where the time goes in v1:
time: 414 us; the launch traced here: 413 us
  waiting for transfers between devices  249 us (60%)
  matrix products  57.5 us (14%)
  local copies, waits for them, and re-layouts  39.1 us (9%)
  other arithmetic  18.8 us (5%)
  blocking collectives  18.6 us (4%)
  starting transfers between devices  16.2 us (4%)
  between operations  13.9 us (3%)
    all_to_all x1, waiting for transfers between devices, number_panel(): arr_now = jax.lax.all_to_all(response, 'ctx', 0, 0)  196 us
    all_gather x1, waiting for transfers between devices, attend_all(): everyone = lax.all_gather(paired[None], 'ctx', axis=0, tiled=True)  29 us
    reduce_scatter x1, waiting for transfers between devices, route_experts(): lax.psum_scatter(jnp.dot(hidden_activation, down_local, preferred_element...  24.5 us
    dot_general x1, matrix products, route_experts(): jnp.dot(hidden_activation, down_local, preferred_element_type=jnp.float32)  21 us
    all_to_all x1, blocking collectives, route_experts(): lax.all_to_all(outgoing, 'exp', split_axis=0, concat_axis=0, tiled=True)  18.6 us
    dot_general x1, matrix products, attend_all(): jnp.einsum('prhgd,pkhd->phgrk', query_head_rows, key_portion, preferred_e...  13.4 us
    reduce_sum x1, other arithmetic, attend_all(): new_sum = jnp.sum(weights, axis=-1)  11.6 us
    dot_general x1, matrix products, attend_all(): jnp.einsum('phgrk,pkhd->phgrd', weights.astype(jnp.bfloat16), value_porti...  10.9 us
  transfers between devices with their start and end apart: 5, of which 3 were waited for; matrix products, arithmetic and copies ran while one was open for 26% of the time, Pallas kernels for 0%

profile of v1, /device:TPU:2, one launch (start us, length us, event | category | flops | bytes accessed | tf_op | source)
XLA Modules:
  0.0 413.3 jit_solution(9780575110425472419)
XLA Ops:
  7.2 1.1 constant_dynamic-update-slice_fusion.1
  10.6 1.3 fusion.24
  13.5 1.4 convolution_convert_fusion.1
  15.4 18.6 %all_to_all.15 = bf16[16,4,5120]{2,1,0:T(4,128)(2,1)S(1)} all-to-all(bf16[16,4,5120]{2,1,0:T(4,128)(2,1)S(1)} %copy.30), channel_id=1, replica_groups=mesh['ctx'=16,'exp'=16] {'exp'}, dimensions={0} | all-to-all | bytes 1310720 | tf_op jit(solution)/shard_map/all_to_all | solution.py:110
  35.0 6.4 %stack.24 = bf16[16,64,5120]{2,1,0:T(8,128)(2,1)} broadcast(bf16[64,5120]{1,0:T(8,128)(2,1)} %stack_reshape.2), dimensions={1,2} | broadcast | bytes 11141120 | tf_op jit(solution)/shard_map/stack | solution.py:17
  41.4 8.7 %all-to-all-start.1 = ((bf16[16,64,5120]{2,1,0:T(8,128)(2,1)}), bf16[16,64,5120]{2,1,0:T(8,128)(2,1)}, u32[]{:S(2)}, u32[]{:S(2)}) async-start(bf16[16,64,5120]{2,1,0:T(8,128)(2,1)} %stack.24), calls=%async_computation.1 | async-start | bytes 20971520 | tf_op jit(solution)/shard_map/all_to_all | solution.py:18
  51.0 29.0 %all-gather.6.cloned.1.call-done = bf16[32,64,1024]{2,1,0:T(8,128)(2,1)} async-done(((bf16[2,64,1024]{2,1,0:T(8,128)(2,1)}), bf16[32,64,1024]{2,1,0:T(8,128)(2,1)}) %all-gather.6.cloned.1.call-update) | async-done | bytes 4194320 | tf_op jit(solution)/shard_map/all_gather | solution.py:39
  80.0 2.8 gather_fusion.1
  83.7 195.6 %all-to-all-done.1 = bf16[16,64,5120]{2,1,0:T(8,128)(2,1)} async-done(((bf16[16,64,5120]{2,1,0:T(8,128)(2,1)}), bf16[16,64,5120]{2,1,0:T(8,128)(2,1)}, u32[]{:S(2)}, u32[]{:S(2)}) %all-to-all-start.1) | async-done | bytes 10485792 | tf_op jit(solution)/shard_map/all_to_all | solution.py:18
  279.3 8.6 %fusion.11 = f32[1024,256]{1,0:T(8,128)} fusion(bf16[1024,5120]{1,0:T(8,128)(2,1)} %bitcast.17, bf16[1,5120,256]{2,1,0:T(8,128)(2,1)} %param.17), kind=kOutput, calls=%fused_computation.20 | convolution fusion | flops 2684354560 | bytes 14155776 | tf_op jit(solution)/shard_map/dot_general | solution.py:112
  287.8 21.0 %convolution_convert_fusion = bf16[1024,5120]{1,0:T(8,128)(2,1)} fusion(bf16[1,256,5120]{2,1,0:T(8,128)(2,1)S(1)} %copy-done, bf16[1024,5120]{1,0:T(8,128)(2,1)} %bitcast.17, bf16[1,5120,256]{2,1,0:T(8,128)(2,1)} %param.18, f32[1024,256]{1,0:T(8,128)} %fusion.11), kind=kOutput, calls=%fused_computation.9 | convolution fusion | flops 5375524864 | bytes 27262976 | tf_op jit(solution)/shard_map/dot_general | solution.py:116
  308.9 1.1 copy-done.5
  311.1 3.9 fusion.57
  315.0 3.9 fusion.7
  319.0 6.3 %copy.25 = bf16[2,2048,512]{1,2,0:T(8,128)(2,1)} copy(bf16[2,2048,512]{2,1,0:T(8,128)(2,1)} %get-tuple-element.3) | data formatting | bytes 8388608 | tf_op jit(solution)/shard_map/slice | solution.py:55
  325.3 6.4 %copy.22 = bf16[2,2048,512]{1,2,0:T(8,128)(2,1)} copy(bf16[2,2048,512]{2,1,0:T(8,128)(2,1)} %get-tuple-element.2) | data formatting | bytes 8388608 | tf_op jit(solution)/shard_map/slice | solution.py:52
  331.6 13.4 %fusion = (f32[2,4,5,64]{3,2,1,0:T(8,128)S(1)}, f32[2,4,2048,64,5]{2,3,4,1,0:T(8,128)}) fusion(pred[2,64,2048]{2,1,0:T(8,128)(4,1)S(1)} %pad_add_fusion, bf16[2,2048,4,128,1]{1,3,4,2,0:T(8,128)(2,1)} %bitcast.71, bf16[2,64,4,5,128]{4,3,2,1,0:T(8,128)(2,1)S(1)} %reshape.252), kind=kOutput, calls=%fused_computation.4 | convolution fusion | flops 1357903360 | bytes 26093568 | tf_op jit(solution)/shard_map/prhgd,pkhd->phgrk/dot_general | solution.py:59
  345.1 11.6 %fusion.1 = f32[2,4,5,64]{3,2,1,0:T(8,128)} fusion(f32[2,4,2048,64,5]{2,3,4,1,0:T(8,128)} %get-tuple-element.7, f32[2,4,5,64]{3,2,1,0:T(8,128)S(1)} %broadcast_maximum_fusion, pred[2,64,2048]{2,1,0:T(8,128)(4,1)S(1)} %pad_add_fusion), kind=kLoop, calls=%fused_computation.5 | loop fusion | flops 26211840 | bytes 21254144 | tf_op jit(solution)/shard_map/reduce_sum | solution.py:73
  356.7 24.5 %reduce-scatter.2.cloned.1.call-done = bf16[64,5120]{1,0:T(8,128)(2,1)} async-done(((bf16[1024,5120]{1,0:T(8,128)(2,1)}), bf16[64,5120]{1,0:T(8,128)(2,1)}) %reduce-scatter.2.cloned.1.call-update) | async-done | bytes 655376 | tf_op jit(solution)/shard_map/reduce_scatter | solution.py:115
  381.2 2.3 reshape.255
  383.5 7.3 %all-to-all-start.2 = ((bf16[16,4,5120]{2,1,0:T(4,128)(2,1)}), bf16[16,4,5120]{2,1,0:T(4,128)(2,1)S(1)}, u32[]{:S(2)}, u32[]{:S(2)}) async-start(bf16[16,4,5120]{2,1,0:T(4,128)(2,1)} %reshape.255), calls=%async_computation.3 | async-start | bytes 1310720 | tf_op jit(solution)/shard_map/all_to_all | solution.py:123
  390.8 10.9 %divide_convert_fusion = bf16[2,64,4,5,128]{4,1,3,2,0:T(8,128)(2,1)S(1)} fusion(bf16[2,2048,4,128,1]{1,3,4,2,0:T(8,128)(2,1)} %bitcast.72, f32[2,4,2048,64,5]{2,3,4,1,0:T(8,128)} %get-tuple-element.7, f32[2,4,5,64]{3,2,1,0:T(8,128)} %copy-done.6, pred[2,64,2048]{2,1,0:T(8,128)(4,1)S(1)} %pad_add_fusion, f32[2,64,4,5]{1,3,2,0:T(8,128)} %bitcast.73), kind=kOutput, calls=%fused_computation.23 | convolution fusion | flops 1369047040 | bytes 26103808 | tf_op jit(solution)/shard_map/phgrk,pkhd->phgrd/dot_general | solution.py:74
  401.7 1.5 copy.27
  403.2 2.6 convert_element_type.51
  (47 shorter events, 9.3 us)
Async XLA Ops:
  7.2 280.7 %copy-start = (bf16[1,256,5120]{2,1,0:T(8,128)(2,1)S(1)}, bf16[1,256,5120]{2,1,0:T(8,128)(2,1)}, u32[]{:S(2)}) copy-start(bf16[1,256,5120]{2,1,0:T(8,128)(2,1)} %param.19) | copy-start | bytes 7864324
  7.2 72.8 %all-gather.6.cloned.1.call-start = ((), (), s32[]{:S(2)}) async-start(), calls=%async_computation.6 | async-start | bytes 4456448 | tf_op jit(solution)/shard_map/all_gather | solution.py:39
  9.2 0.7 copy-start.3
  41.4 8.9 %copy-start.2 = (s32[32]{0:T(128)S(1)}, s32[32]{0:T(128)}, u32[]{:S(2)}) copy-start(s32[32]{0:T(128)} %param.13) | copy-start | bytes 388
  41.4 41.3 %copy-start.4 = (bf16[2,64,1024]{2,1,0:T(8,128)(2,1)S(1)}, bf16[2,64,1024]{2,1,0:T(8,128)(2,1)}, u32[]{:S(2)}) copy-start(bf16[2,64,1024]{2,1,0:T(8,128)(2,1)} %copy-done.3) | copy-start | bytes 786436
  41.4 237.9 %all-to-all-start.1 = ((bf16[16,64,5120]{2,1,0:T(8,128)(2,1)}), bf16[16,64,5120]{2,1,0:T(8,128)(2,1)}, u32[]{:S(2)}, u32[]{:S(2)}) async-start(bf16[16,64,5120]{2,1,0:T(8,128)(2,1)} %stack.24), calls=%async_computation.1 | async-start | bytes 20971520 | tf_op jit(solution)/shard_map/all_to_all | solution.py:18
  50.2 260.9 %all-gather.4.cloned.1.call-start = ((), (), s32[]{:S(2)}) async-start(), calls=%async_computation.4 | async-start | bytes 8912896 | tf_op jit(solution)/shard_map/all_gather | solution.py:46
  83.6 297.5 %reduce-scatter.2.cloned.1.call-start = ((), (), s32[]{:S(2)}) async-start(), calls=%async_computation.5 | async-start | bytes 11141120 | tf_op jit(solution)/shard_map/reduce_scatter | solution.py:115
  308.8 1.1 copy-start.5
  345.1 11.6 %copy-start.6 = (f32[2,4,5,64]{3,2,1,0:T(8,128)}, f32[2,4,5,64]{3,2,1,0:T(8,128)S(1)}, u32[]{:S(2)}) copy-start(f32[2,4,5,64]{3,2,1,0:T(8,128)S(1)} %broadcast_maximum_fusion) | copy-start | bytes 30724
  383.5 22.2 %all-to-all-start.2 = ((bf16[16,4,5120]{2,1,0:T(4,128)(2,1)}), bf16[16,4,5120]{2,1,0:T(4,128)(2,1)S(1)}, u32[]{:S(2)}, u32[]{:S(2)}) async-start(bf16[16,4,5120]{2,1,0:T(4,128)(2,1)} %reshape.255), calls=%async_computation.3 | async-start | bytes 1310720 | tf_op jit(solution)/shard_map/all_to_all | solution.py:123
  390.8 16.0 %copy-start.1 = (bf16[1,256,5120]{2,1,0:T(8,128)(2,1)S(1)}, bf16[1,256,5120]{2,1,0:T(8,128)(2,1)}, u32[]{:S(2)}) copy-start(bf16[1,256,5120]{2,1,0:T(8,128)(2,1)} %param.19) | copy-start | bytes 7864324
Sparse Core Ops, SparseCore 0:
  10.4 69.5 all-gather.5
  83.7 84.0 all-gather.3
  309.0 72.1 reduce-scatter.1
